TPU v7x, 32 devices: a whole 2x2x4 slice. The times are simulated.
32 devices in a mesh: grp: 2 (over y), wide: 8 (over z, x), narrow: 2 (over core).
Axes of the slice: x: 2, y: 2, z: 4, core: 2. Of those that a mesh axis runs over, the one named last changes fastest.
Arguments:
- denoised: float32 [4, 512, 512], P('grp', 'wide', 'narrow'), parts along dimension 0, may hold values from -6 to 6
- clean_volume: float32 [4, 512, 512], P('grp', 'wide', 'narrow'), parts along dimension 0, may hold values from -6 to 6
- weight: float32 [512, 512], P(('wide', 'narrow')), may hold values from 0.1 to 2
- act_in: bfloat16 [64, 4, 512, 512], P(None, 'grp', 'wide', 'narrow'), parts along dimension 1, may hold values from -6 to 6
- act_mid: bfloat16 [64, 4, 512, 512], P(None, 'grp', 'wide', 'narrow'), parts along dimension 1, as said below
- w_first: bfloat16 [27, 64, 64], replicated, may hold values from -0.15625 to 0.15625
- w_second: bfloat16 [27, 64], replicated, may hold values from -0.15625 to 0.15625
Outputs:
- grad_in: bfloat16 [64, 4, 512, 512], P(None, 'grp', 'wide', 'narrow'), parts along dimension 1
- grad_first: float32 [54, 64, 64], P('grp'), parts along dimension 0
- grad_second: float32 [54, 64], P('grp'), parts along dimension 0
There are 2 independent parts, one for each index of `grp`. A program takes and returns all parts, laid end to end along the dimension named above; an argument that names none is the same for every part. Nothing has to cross between parts.
Inputs may be any that keep to these rules, and one draw needn't show every extreme that they name: act_mid is a rectifier's output: non-negative, with many zeros.
All inputs are finite; a program needn't handle non-finite values.
Results may differ from a plain program's by a relative error of at most 0.0058.
Values may be sent and summed in bfloat16 or wider, within the bound.
No kernel may reach another device: no remote copies, remote signals or barrier semaphores. Data moves between devices by JAX's collectives and lax.ppermute only.
A program may use at most 320 MiB of HBM per device.

v0:
```python
import jax
import jax.numpy as jnp
from jax import lax
from jax.sharding import PartitionSpec as P

two_pi = 6.283185307179586
highest = lax.Precision.HIGHEST


def with_halo(x, sides, width):
    for axis, dim in sides:
        devices, length = (lax.axis_size(axis), x.shape[dim])
        up = [(i, (i + 1) % devices) for i in range(devices - 1)]
        down = [(j, i) for i, j in up]
        last = lax.slice_in_dim(x, length - width, length, axis=dim)
        first = lax.slice_in_dim(x, 0, width, axis=dim)
        before = lax.ppermute(last, axis, up)
        after = lax.ppermute(first, axis, down)
        x = jnp.concatenate([before, x, after], axis=dim)
    return x


def phase_table(left_index, right_index, length):
    product = left_index[:, None] * right_index[None, :] % length
    angles = product.astype(jnp.float32) * (two_pi / length)
    return (jnp.cos(angles), jnp.sin(angles))


def shifted_windows(padded, slices, rows_x, cols_y, taps_list):
    windows = []
    for tap_index in taps_list:
        step_z = tap_index // 9 - 1
        step_x = tap_index // 3 % 3 - 1
        step_y = tap_index % 3 - 1
        windows.append(
            padded[
                ...,
                1 - step_z : 1 - step_z + slices,
                1 - step_x : 1 - step_x + rows_x,
                1 - step_y : 1 - step_y + cols_y,
            ]
        )
    return jnp.stack(windows, axis=0)


def shards(denoised, clean_volume, weight, act_in, act_mid, w_first, w_second):
    wide_count = lax.axis_size("wide")
    narrow_count = lax.axis_size("narrow")
    slices, rows_x, half_cols = denoised.shape
    total_y = half_cols * narrow_count
    total_x = rows_x * wide_count
    kept_cols = half_cols // wide_count
    narrow_index = lax.axis_index("narrow")
    error_field = denoised - clean_volume
    columns = lax.iota(jnp.int32, total_y)
    frequency = (
        columns % half_cols // kept_cols * narrow_count + columns // half_cols
    ) * kept_cols + columns % kept_cols
    own_rows = narrow_index * half_cols + lax.iota(jnp.int32, half_cols)
    cos_y, sin_y = phase_table(own_rows, frequency, total_y)
    part_real = jnp.einsum("zxy,yc->zxc", error_field, cos_y, precision=highest)
    part_imag = -jnp.einsum("zxy,yc->zxc", error_field, sin_y, precision=highest)
    spec_real, spec_imag = (
        lax.psum_scatter(part_real, "narrow", scatter_dimension=2, tiled=True),
        lax.psum_scatter(part_imag, "narrow", scatter_dimension=2, tiled=True),
    )
    positions = lax.iota(jnp.int32, total_x)
    cos_x, sin_x = phase_table(positions, positions, total_x)
    pieces = (
        lax.all_to_all(
            spec_real.reshape(slices, rows_x, wide_count, kept_cols),
            "wide",
            split_axis=2,
            concat_axis=1,
            tiled=True,
        ),
        lax.all_to_all(
            spec_imag.reshape(slices, rows_x, wide_count, kept_cols),
            "wide",
            split_axis=2,
            concat_axis=1,
            tiled=True,
        ),
    )
    item_count = pieces[0].shape[0]
    in_real = pieces[0].reshape(item_count, total_x, kept_cols)
    in_imag = pieces[1].reshape(item_count, total_x, kept_cols)
    four_real = jnp.einsum("mxk,xq->mkq", in_real, cos_x, precision=highest) + jnp.einsum(
        "mxk,xq->mkq", in_imag, sin_x, precision=highest
    )
    four_imag = jnp.einsum("mxk,xq->mkq", in_imag, cos_x, precision=highest) - jnp.einsum(
        "mxk,xq->mkq", in_real, sin_x, precision=highest
    )
    weighted_real = weight * four_real
    weighted_imag = weight * four_imag
    out_real = jnp.einsum("mkq,qx->mxk", weighted_real, cos_x, precision=highest) - jnp.einsum(
        "mkq,qx->mxk", weighted_imag, sin_x, precision=highest
    )
    out_imag = jnp.einsum("mkq,qx->mxk", weighted_imag, cos_x, precision=highest) + jnp.einsum(
        "mkq,qx->mxk", weighted_real, sin_x, precision=highest
    )
    back_real = lax.all_to_all(
        out_real.reshape(item_count, wide_count, rows_x, kept_cols),
        "wide",
        split_axis=1,
        concat_axis=3,
        tiled=True,
    ).reshape(item_count, rows_x, half_cols)
    back_imag = lax.all_to_all(
        out_imag.reshape(item_count, wide_count, rows_x, kept_cols),
        "wide",
        split_axis=1,
        concat_axis=3,
        tiled=True,
    ).reshape(item_count, rows_x, half_cols)
    local_cols = lax.iota(jnp.int32, half_cols)
    own_freq = (
        local_cols // kept_cols * narrow_count + narrow_index
    ) * kept_cols + local_cols % kept_cols
    cos_back, sin_back = phase_table(own_freq, columns, total_y)
    part_term = jnp.einsum("zxc,cy->zxy", back_real, cos_back, precision=highest) - jnp.einsum(
        "zxc,cy->zxy", back_imag, sin_back, precision=highest
    )
    field_real = lax.psum_scatter(part_term, "narrow", scatter_dimension=2, tiled=True)
    grad_noise = (field_real * (-2.0 / (total_x * total_y))).astype(jnp.bfloat16)
    noise_rim = with_halo(grad_noise, (("wide", 1), ("narrow", 2)), 1)
    noise_pad = jnp.pad(noise_rim, ((1, 1), (0, 0), (0, 0)))
    noise_windows = shifted_windows(noise_pad, slices, rows_x, half_cols, range(27))
    grad_mid = jnp.einsum(
        "tc,tzxy->czxy", w_second, noise_windows, preferred_element_type=jnp.float32
    )
    masked = jnp.where(act_mid > 0, grad_mid, 0.0).astype(jnp.bfloat16)
    masked_rim = with_halo(masked, (("wide", 2), ("narrow", 3)), 1)
    grad_second = jnp.einsum(
        "czxy,tzxy->tc", act_mid, noise_windows, preferred_element_type=jnp.float32
    )
    masked_pad = jnp.pad(masked_rim, ((0, 0), (1, 1), (0, 0), (0, 0)))
    channels = act_in.shape[0]
    grad_in = jnp.zeros(act_in.shape, jnp.float32)
    first_parts = []
    for plane_index in range(9):
        stacked = shifted_windows(
            masked_pad, slices, rows_x, half_cols, [plane_index, plane_index + 9, plane_index + 18]
        )
        first_parts.append(
            jnp.einsum("izxy,dozxy->dio", act_in, stacked, preferred_element_type=jnp.float32)
        )
        grad_in = grad_in + jnp.einsum(
            "dio,dozxy->izxy", w_first[plane_index::9], stacked, preferred_element_type=jnp.float32
        )
    grad_first = jnp.stack(first_parts, axis=1).reshape(27, channels, channels)
    grad_first, grad_second = lax.psum((grad_first, grad_second), ("wide", "narrow"))
    return (grad_in.astype(jnp.bfloat16), grad_first, grad_second)


def solution(mesh):
    placed = (
        P("grp", "wide", "narrow"),
        P("grp", "wide", "narrow"),
        P(("wide", "narrow"), None),
        P(None, "grp", "wide", "narrow"),
        P(None, "grp", "wide", "narrow"),
        P(),
        P(),
    )
    return jax.shard_map(
        shards,
        mesh=mesh,
        in_specs=placed,
        out_specs=(P(None, "grp", "wide", "narrow"), P("grp", None, None), P("grp", None)),
        check_vma=False,
    )
```

profile of v0, /device:TPU:0, one launch (start us, length us, event | category | flops | bytes accessed | tf_op | source)
XLA Modules:
  0.0 590.2 jit_solution(6544291308981167660)
XLA Ops:
  15.5 6.4 %reduce-scatter.4.cloned.1.call-done = f32[2,64,256]{2,1,0:T(8,128)} async-done(((f32[2,64,512]{2,1,0:T(8,128)}), f32[2,64,256]{2,1,0:T(8,128)}) %reduce-scatter.4.cloned.1.call-update) | async-done | bytes 131088 | tf_op jit(solution)/shard_map/reduce_scatter | solution.py:64
  23.8 5.7 all-to-all-start
  80.5 5.2 all-to-all-start.2
  98.9 6.0 %all-to-all-done.3 = f32[8,1,4096]{2,1,0:T(1,128)S(1)} async-done(((f32[8,1,4096]{2,1,0:T(1,128)}), f32[8,1,4096]{2,1,0:T(1,128)S(1)}, u32[]{:S(2)}, u32[]{:S(2)}) %all-to-all-start.3) | async-done | bytes 131104 | tf_op jit(solution)/shard_map/all_to_all | solution.py:109
  111.8 5.5 reduce-scatter.8.cloned.1.call-done
  147.6 6.3 %fusion.100 = f32[27,64]{1,0:T(8,128)S(1)} fusion(bf16[64,2,64,256]{3,2,1,0:T(8,128)(2,1)S(1)} %copy-done.27, bf16[27,2,64,256]{3,2,1,0:T(8,128)(2,1)S(1)} %constant_dynamic-update-slice_fusion), kind=kOutput, calls=%fused_computation.124 | convolution fusion | flops 113246208 | bytes 5970688 | tf_op jit(solution)/shard_map/czxy,tzxy->tc/dot_general | solution.py:134
  154.0 60.0 %psum.15 = f32[27,64]{1,0:T(8,128)} all-reduce(f32[27,64]{1,0:T(8,128)S(1)} %fusion.100), channel_id=1, replica_groups=mesh['grp'=2,'wide'=8,'narrow'=2] {'wide','narrow'}, use_global_device_ids=true, to_apply=%region_4.5 | all-reduce | flops 1728 | bytes 13824 | tf_op jit(solution)/shard_map/psum | solution.py:152
  227.9 5.8 fusion.27
  242.7 8.2 %pad_maximum_fusion.9 = (bf16[64,2,66,257]{3,0,2,1:T(8,128)(2,1)S(1)}, bf16[64,2,66,257]{3,0,2,1:T(8,128)(2,1)S(1)}) fusion(bf16[64,2,66,1]{3,0,2,1:T(8,128)(2,1)} %copy.104, bf16[64,2,1,256]{3,0,2,1:T(8,128)(2,1)S(1)} %collective-permute-done.5, bf16[64,2,64,256]{3,0,2,1:T(8,128)(2,1)} %copy-done.2, bf16[64,2,1,256]{3,0,2,1:T(8,128)(2,1)S(1)} %collective-permute-done.4, ...), kind=kLoop, calls=%fused_computation.30 | loop fusion | flops 34738176 | bytes 13043712 | tf_op jit(solution)/shard_map/concatenate | solution.py:19
  250.9 9.2 %slice_bitcast_fusion.22 = (bf16[1,64,2,64,256]{4,1,3,2,0:T(8,128)(2,1)}, bf16[1,64,2,64,256]{4,1,3,2,0:T(8,128)(2,1)}, bf16[1,64,2,64,256]{4,1,3,2,0:T(8,128)(2,1)}) fusion(bf16[64,2,66,257]{3,0,2,1:T(8,128)(2,1)S(1)} %get-tuple-element.36), kind=kLoop, calls=%fused_computation.77 | loop fusion | bytes 25165824 | tf_op jit(solution)/shard_map/stack | solution.py:43
  260.1 8.9 %select_maximum_fusion = bf16[64,4,66,258]{3,0,2,1:T(8,128)(2,1)} fusion(bf16[64,2,66,1]{3,0,2,1:T(8,128)(2,1)} %copy.104, bf16[64,2,66,1]{3,0,2,1:T(8,128)(2,1)S(1)} %copy-done.4, bf16[64,2,1,256]{3,0,2,1:T(8,128)(2,1)S(1)} %collective-permute-done.5, bf16[64,2,64,256]{3,0,2,1:T(8,128)(2,1)S(1)} %copy-done.3, ...), kind=kLoop, calls=%fused_computation.3 | loop fusion | flops 78465024 | bytes 13077504 | tf_op jit(solution)/shard_map/concatenate | solution.py:19
  269.1 64.1 %slice_bitcast_fusion.23 = (bf16[1,64,2,64,256]{4,1,3,2,0:T(8,128)(2,1)}, bf16[1,64,2,64,256]{4,1,3,2,0:T(8,128)(2,1)}, bf16[1,64,2,64,256]{4,1,3,2,0:T(8,128)(2...) fusion(bf16[64,4,66,258]{3,0,2,1:T(8,128)(2,1)} %select_maximum, ...), kind=kLoop, calls=%fused_computation.78 | loop fusion | bytes 150994944 | tf_op jit(solution)/shard_map/stack | solution.py:43
  333.2 15.3 %fusion.49 = f32[3,9,64,64]{2,3,0,1:T(8,128)} fusion(bf16[1,64,2,64,256]{4,1,3,2,0:T(8,128)(2,1)} %get-tuple-element.28, bf16[1,64,2,64,256]{4,1,3,2,0:T(8,128)(2,1)} %get-tuple-element.30, bf16[1,64,2,64,256]{4,1,3,2,0:T(8,128)(2,1)} %get-tuple-element.12, bf16[64,2,64,256,1]{3,2,1,0,4:T(8,128)(2,1)} %bitcast.559), kind=kOutput, calls=%fused_computation.107 | convolution fusion | flops 817889280 | bytes 16875520 | tf_op jit(solution)/shard_map/izxy,dozxy->dio/dot_general | solution.py:146
  348.6 8.5 %fusion.25 = f32[2,64,256,64,1]{2,3,1,0,4:T(8,128)} fusion(bf16[1,64,2,64,256]{4,1,3,2,0:T(8,128)(2,1)} %get-tuple-element.28, bf16[1,64,2,64,256]{4,1,3,2,0:T(8,128)(2,1)} %get-tuple-element.30, bf16[1,64,2,64,256]{4,1,3,2,0:T(8,128)(2,1)} %get-tuple-element.12, bf16[27,64,64]{2,1,0:T(8,128)(2,1)S(1)} %copy-done.29), kind=kOutput, calls=%fused_computation.49 | convolution fusion | flops 843055104 | bytes 21020672 | tf_op jit(solution)/shard_map/dio,dozxy->izxy/dot_general | solution.py:148
  359.8 5.2 fusion.23
  365.0 9.2 %fusion.55 = f32[3,9,64,64]{2,3,0,1:T(8,128)} fusion(f32[3,9,64,64]{2,3,0,1:T(8,128)} %fusion.49, bf16[1,64,2,64,256]{4,1,3,2,0:T(8,128)(2,1)S(1)} %copy-done.21, bf16[1,64,2,64,256]{4,1,3,2,0:T(8,128)(2,1)S(1)} %copy-done.10, bf16[1,64,2,64,256]{4,1,3,2,0:T(8,128)(2,1)S(1)} %copy-done.22, bf16[64,2,64,256,1]{3,2,1,0,4:T(8,128)(2,1)} %bitcast.560), kind=kOutput, calls=%fused_computation.109 | convolution fusion | flops 817889280 | bytes 16875520 | tf_op jit(solution)/shard_map/izxy,dozxy->dio/dot_general | solution.py:146
  381.7 5.5 fusion.21
  387.2 10.4 %fusion.61 = f32[3,9,64,64]{2,3,0,1:T(8,128)} fusion(f32[3,9,64,64]{2,3,0,1:T(8,128)} %fusion.55, bf16[1,64,2,64,256]{4,1,3,2,0:T(8,128)(2,1)S(1)} %copy-done.19, bf16[1,64,2,64,256]{4,1,3,2,0:T(8,128)(2,1)} %copy-done.26, bf16[1,64,2,64,256]{4,1,3,2,0:T(8,128)(2,1)S(1)} %copy-done.20, bf16[64,2,64,256,1]{3,2,1,0,4:T(8,128)(2,1)} %bitcast.561), kind=kOutput, calls=%fused_computation.111 | convolution fusion | flops 817889280 | bytes 16875520 | tf_op jit(solution)/shard_map/izxy,dozxy->dio/dot_general | solution.py:146
  397.6 6.5 %fusion.19 = f32[2,64,256,64,1]{2,3,1,0,4:T(8,128)} fusion(bf16[1,64,2,64,256]{4,1,3,2,0:T(8,128)(2,1)S(1)} %copy-done.17, bf16[1,64,2,64,256]{4,1,3,2,0:T(8,128)(2,1)} %get-tuple-element.32, bf16[1,64,2,64,256]{4,1,3,2,0:T(8,128)(2,1)S(1)} %copy-done.18, bf16[27,64,64]{2,1,0:T(8,128)(2,1)S(1)} %copy-done.29), kind=kOutput, calls=%fused_computation.43 | convolution fusion | flops 843055104 | bytes 21020672 | tf_op jit(solution)/shard_map/dio,dozxy->izxy/dot_general | solution.py:148
  404.2 10.4 %fusion.67 = f32[3,9,64,64]{2,3,0,1:T(8,128)} fusion(f32[3,9,64,64]{2,3,0,1:T(8,128)} %fusion.61, bf16[1,64,2,64,256]{4,1,3,2,0:T(8,128)(2,1)S(1)} %copy-done.17, bf16[1,64,2,64,256]{4,1,3,2,0:T(8,128)(2,1)} %get-tuple-element.32, bf16[1,64,2,64,256]{4,1,3,2,0:T(8,128)(2,1)S(1)} %copy-done.18, bf16[64,2,64,256,1]{3,2,1,0,4:T(8,128)(2,1)} %bitcast.562), kind=kOutput, calls=%fused_computation.113 | convolution fusion | flops 817889280 | bytes 16875520 | tf_op jit(solution)/shard_map/izxy,dozxy->dio/dot_general | solution.py:146
  414.6 5.3 fusion.17
  420.0 9.3 %fusion.73 = f32[3,9,64,64]{2,3,0,1:T(8,128)} fusion(f32[3,9,64,64]{2,3,0,1:T(8,128)} %fusion.67, bf16[1,64,2,64,256]{4,1,3,2,0:T(8,128)(2,1)S(1)} %copy-done.15, bf16[1,64,2,64,256]{4,1,3,2,0:T(8,128)(2,1)S(1)} %bitcast.549, bf16[1,64,2,64,256]{4,1,3,2,0:T(8,128)(2,1)S(1)} %copy-done.16, bf16[64,2,64,256,1]{3,2,1,0,4:T(8,128)(2,1)} %bitcast.563), kind=kOutput, calls=%fused_computation.115 | convolution fusion | flops 817889280 | bytes 16875520 | tf_op jit(solution)/shard_map/izxy,dozxy->dio/dot_general | solution.py:146
  429.3 6.6 %fusion.15 = f32[2,64,256,64,1]{2,3,1,0,4:T(8,128)} fusion(bf16[1,64,2,64,256]{4,1,3,2,0:T(8,128)(2,1)S(1)} %copy-done.13, bf16[1,64,2,64,256]{4,1,3,2,0:T(8,128)(2,1)} %get-tuple-element.35, bf16[1,64,2,64,256]{4,1,3,2,0:T(8,128)(2,1)S(1)} %copy-done.14, bf16[27,64,64]{2,1,0:T(8,128)(2,1)S(1)} %copy-done.29), kind=kOutput, calls=%fused_computation.39 | convolution fusion | flops 843055104 | bytes 21020672 | tf_op jit(solution)/shard_map/dio,dozxy->izxy/dot_general | solution.py:148
  436.0 10.4 %fusion.79 = f32[3,9,64,64]{2,3,0,1:T(8,128)} fusion(f32[3,9,64,64]{2,3,0,1:T(8,128)} %fusion.73, bf16[1,64,2,64,256]{4,1,3,2,0:T(8,128)(2,1)S(1)} %copy-done.13, bf16[1,64,2,64,256]{4,1,3,2,0:T(8,128)(2,1)} %get-tuple-element.35, bf16[1,64,2,64,256]{4,1,3,2,0:T(8,128)(2,1)S(1)} %copy-done.14, bf16[64,2,64,256,1]{3,2,1,0,4:T(8,128)(2,1)} %bitcast.564), kind=kOutput, calls=%fused_computation.117 | convolution fusion | flops 817889280 | bytes 16875520 | tf_op jit(solution)/shard_map/izxy,dozxy->dio/dot_general | solution.py:146
  446.4 5.3 fusion.13
  451.8 9.3 %fusion.85 = f32[3,9,64,64]{2,3,0,1:T(8,128)} fusion(f32[3,9,64,64]{2,3,0,1:T(8,128)} %fusion.79, bf16[1,64,2,64,256]{4,1,3,2,0:T(8,128)(2,1)S(1)} %copy-done.11, bf16[1,64,2,64,256]{4,1,3,2,0:T(8,128)(2,1)S(1)} %copy-done.24, bf16[1,64,2,64,256]{4,1,3,2,0:T(8,128)(2,1)S(1)} %copy-done.12, bf16[64,2,64,256,1]{3,2,1,0,4:T(8,128)(2,1)} %bitcast.565), kind=kOutput, calls=%fused_computation.119 | convolution fusion | flops 817889280 | bytes 16875520 | tf_op jit(solution)/shard_map/izxy,dozxy->dio/dot_general | solution.py:146
  461.2 5.5 fusion.11
  466.7 9.3 %fusion.91 = f32[3,9,64,64]{2,3,0,1:T(8,128)} fusion(f32[3,9,64,64]{2,3,0,1:T(8,128)} %fusion.85, bf16[1,64,2,64,256]{4,1,3,2,0:T(8,128)(2,1)S(1)} %copy-done.8, bf16[1,64,2,64,256]{4,1,3,2,0:T(8,128)(2,1)S(1)} %copy-done.5, bf16[1,64,2,64,256]{4,1,3,2,0:T(8,128)(2,1)S(1)} %copy-done.9, bf16[64,2,64,256,1]{3,2,1,0,4:T(8,128)(2,1)} %bitcast.566), kind=kOutput, calls=%fused_computation.121 | convolution fusion | flops 817889280 | bytes 16875520 | tf_op jit(solution)/shard_map/izxy,dozxy->dio/dot_general | solution.py:146
  476.0 5.2 fusion.9
  481.3 6.4 %fusion.97 = f32[3,9,64,64]{2,3,0,1:T(8,128)} fusion(f32[3,9,64,64]{2,3,0,1:T(8,128)} %fusion.91, bf16[1,64,2,64,256]{4,1,3,2,0:T(8,128)(2,1)S(1)} %copy-done.7, bf16[1,64,2,64,256]{4,1,3,2,0:T(8,128)(2,1)S(1)} %copy-done.25, bf16[1,64,2,64,256]{4,1,3,2,0:T(8,128)(2,1)S(1)} %copy-done.6, bf16[64,2,64,256,1]{3,2,1,0,4:T(8,128)(2,1)S(1)} %bitcast.567), kind=kOutput, calls=%fused_computation.123 | convolution fusion | flops 817889280 | bytes 16875520 | tf_op jit(solution)/shard_map/izxy,dozxy->dio/dot_general | solution.py:146
  490.1 25.0 %fusion.39 = bf16[64,2,64,256]{3,0,1,2:T(8,128)(2,1)S(1)} fusion(f32[2,64,256,64,1]{2,3,1,0,4:T(8,128)} %fusion.9, f32[2,64,256,64,1]{2,3,1,0,4:T(8,128)} %fusion.11, f32[2,64,256,64,1]{2,3,1,0,4:T(8,128)} %fusion.13, f32[2,64,256,64,1]{2,3,1,0,4:T(8,128)} %fusion.15, f32[2,64,256,64,1]{2,3,1,0,4:T(8,128)} %fusion.17, f32[2,64,256,64,1]{2,3,1,0,4:T(8,128)} %fusion.19, ...), kind=kLoop, calls=%fused_computation.90 | loop fusion | flops 18874368 | bytes 79691776 | tf_op jit(solution)/shard_map/convert_element_type | solution.py:153
  519.6 61.7 %all-reduce.4.cloned.1.call-done = f32[27,64,64]{2,1,0:T(8,128)} async-done(((f32[27,64,64]{2,1,0:T(8,128)}), f32[27,64,64]{2,1,0:T(8,128)}) %all-reduce.4.cloned.1.call-update) | async-done | bytes 442384 | tf_op jit(solution)/shard_map/psum | solution.py:152
  (183 shorter events, 153.3 us)
Async XLA Ops:
  7.2 128.0 %copy-start = (bf16[27,64]{1,0:T(8,128)(2,1)S(1)}, bf16[27,64]{1,0:T(8,128)(2,1)}, u32[]{:S(2)}) copy-start(bf16[27,64]{1,0:T(8,128)(2,1)} %param.13) | copy-start | bytes 10372
  7.2 14.7 %reduce-scatter.4.cloned.1.call-start = ((), (), s32[]{:S(2)}) async-start(), calls=%async_computation.7 | async-start | bytes 393216 | tf_op jit(solution)/shard_map/reduce_scatter | solution.py:64
  11.4 22.3 %reduce-scatter.6.cloned.1.call-start = ((), (), s32[]{:S(2)}) async-start(), calls=%async_computation.8 | async-start | bytes 393216 | tf_op jit(solution)/shard_map/reduce_scatter | solution.py:65
  23.8 13.2 %all-to-all-start = ((f32[8,1,4096]{2,1,0:T(1,128)}), f32[8,1,4096]{2,1,0:T(1,128)S(1)}, u32[]{:S(2)}, u32[]{:S(2)}) async-start(f32[8,1,4096]{2,1,0:T(1,128)} %reshape.165), calls=%async_computation.1 | async-start | bytes 262144 | tf_op jit(solution)/shard_map/all_to_all | solution.py:70
  37.0 12.2 %all-to-all-start.1 = ((f32[8,1,4096]{2,1,0:T(1,128)}), f32[8,1,4096]{2,1,0:T(1,128)S(1)}, u32[]{:S(2)}, u32[]{:S(2)}) async-start(f32[8,1,4096]{2,1,0:T(1,128)} %reshape.167), calls=%async_computation.3 | async-start | bytes 262144 | tf_op jit(solution)/shard_map/all_to_all | solution.py:77
  80.5 12.6 %all-to-all-start.2 = ((f32[8,1,4096]{2,1,0:T(1,128)}), f32[8,1,4096]{2,1,0:T(1,128)S(1)}, u32[]{:S(2)}, u32[]{:S(2)}) async-start(f32[8,1,4096]{2,1,0:T(1,128)} %reshape.169), calls=%async_computation.4 | async-start | bytes 262144 | tf_op jit(solution)/shard_map/all_to_all | solution.py:102
  93.1 11.8 %all-to-all-start.3 = ((f32[8,1,4096]{2,1,0:T(1,128)}), f32[8,1,4096]{2,1,0:T(1,128)S(1)}, u32[]{:S(2)}, u32[]{:S(2)}) async-start(f32[8,1,4096]{2,1,0:T(1,128)} %reshape.171), calls=%async_computation.5 | async-start | bytes 262144 | tf_op jit(solution)/shard_map/all_to_all | solution.py:109
  97.5 19.8 %reduce-scatter.8.cloned.1.call-start = ((), (), s32[]{:S(2)}) async-start(), calls=%async_computation.9 | async-start | bytes 393216 | tf_op jit(solution)/shard_map/reduce_scatter | solution.py:124
  111.7 469.5 %all-reduce.4.cloned.1.call-start = ((), (), s32[]{:S(2)}) async-start(), calls=%async_computation.10 | async-start | bytes 1769472 | tf_op jit(solution)/shard_map/psum | solution.py:152
  117.3 17.8 %copy-start.27 = (bf16[64,2,64,256]{3,2,1,0:T(8,128)(2,1)S(1)}, bf16[64,2,64,256]{3,2,1,0:T(8,128)(2,1)}, u32[]{:S(2)}) copy-start(bf16[64,2,64,256]{3,2,1,0:T(8,128)(2,1)} %param.11) | copy-start | bytes 12582916
  118.4 5.1 collective-permute-start
  122.2 5.5 collective-permute-start.1
  127.8 2.6 collective-permute-start.2
  129.1 3.1 collective-permute-start.3
  141.7 72.4 %collective-permute-start.4 = (bf16[64,2,1,256]{3,0,2,1:T(8,128)(2,1)S(1)}, bf16[64,2,1,256]{3,0,2,1:T(8,128)(2,1)S(1)}, u32[]{:S(2)}, u32[]{:S(2)}) collective-permute-start(bf16[64,2,1,256]{3,0,2,1:T(8,128)(2,1)S(1)} %get-tuple-element.42), channel_id=1, source_target_pairs={{0,2},{2,4},{4,6},{6,8},{8,10},{10,12},{12,14},{1,3},{3,5},{5,7},{... | collective-permute-start | bytes 196616 | tf_op jit(solution)/shard_map/ppermute | solution.py:17
  145.9 68.1 %collective-permute-start.5 = (bf16[64,2,1,256]{3,0,2,1:T(8,128)(2,1)S(1)}, bf16[64,2,1,256]{3,0,2,1:T(8,128)(2,1)S(1)}, u32[]{:S(2)}, u32[]{:S(2)}) collective-permute-start(bf16[64,2,1,256]{3,0,2,1:T(8,128)(2,1)S(1)} %get-tuple-element.43), channel_id=1, source_target_pairs={{2,0},{4,2},{6,4},{8,6},{10,8},{12,10},{14,12},{3,1},{5,3},{7,5},{... | collective-permute-start | bytes 196616 | tf_op jit(solution)/shard_map/ppermute | solution.py:18
  222.6 11.1 %collective-permute-start.6 = (bf16[64,2,66,1]{2,0,3,1:T(8,128)(2,1)S(1)}, bf16[64,2,66,1]{2,0,3,1:T(8,128)(2,1)S(1)}, u32[]{:S(2)}, u32[]{:S(2)}) collective-permute-start(bf16[64,2,66,1]{2,0,3,1:T(8,128)(2,1)S(1)} %copy.101), channel_id=1, source_target_pairs={{0,1},{2,3},{4,5},{6,7},{8,9},{10,11},{12,13},{14,15},{16,17},{18,... | collective-permute-start | bytes 50696 | tf_op jit(solution)/shard_map/ppermute | solution.py:17
  226.4 11.8 %collective-permute-start.7 = (bf16[64,2,66,1]{2,0,3,1:T(8,128)(2,1)S(1)}, bf16[64,2,66,1]{2,0,3,1:T(8,128)(2,1)S(1)}, u32[]{:S(2)}, u32[]{:S(2)}) collective-permute-start(bf16[64,2,66,1]{2,0,3,1:T(8,128)(2,1)S(1)} %copy.102), channel_id=1, source_target_pairs={{1,0},{3,2},{5,4},{7,6},{9,8},{11,10},{13,12},{15,14},{17,16},{19,... | collective-permute-start | bytes 50696 | tf_op jit(solution)/shard_map/ppermute | solution.py:18
  333.2 15.4 %copy-start.29 = (bf16[27,64,64]{2,1,0:T(8,128)(2,1)S(1)}, bf16[27,64,64]{2,1,0:T(8,128)(2,1)}, u32[]{:S(2)}) copy-start(bf16[27,64,64]{2,1,0:T(8,128)(2,1)} %param.12) | copy-start | bytes 663556
  348.6 10.0 %copy-start.21 = (bf16[1,64,2,64,256]{4,1,3,2,0:T(8,128)(2,1)S(1)}, bf16[1,64,2,64,256]{4,1,3,2,0:T(8,128)(2,1)}, u32[]{:S(2)}) copy-start(bf16[1,64,2,64,256]{4,1,3,2,0:T(8,128)(2,1)} %get-tuple-element.26) | copy-start | bytes 12582916
  348.6 11.2 %copy-start.22 = (bf16[1,64,2,64,256]{4,1,3,2,0:T(8,128)(2,1)S(1)}, bf16[1,64,2,64,256]{4,1,3,2,0:T(8,128)(2,1)}, u32[]{:S(2)}) copy-start(bf16[1,64,2,64,256]{4,1,3,2,0:T(8,128)(2,1)} %get-tuple-element.27) | copy-start | bytes 12582916
  387.2 10.4 %copy-start.17 = (bf16[1,64,2,64,256]{4,1,3,2,0:T(8,128)(2,1)S(1)}, bf16[1,64,2,64,256]{4,1,3,2,0:T(8,128)(2,1)}, u32[]{:S(2)}) copy-start(bf16[1,64,2,64,256]{4,1,3,2,0:T(8,128)(2,1)} %get-tuple-element.22) | copy-start | bytes 12582916
  387.2 10.4 %copy-start.18 = (bf16[1,64,2,64,256]{4,1,3,2,0:T(8,128)(2,1)S(1)}, bf16[1,64,2,64,256]{4,1,3,2,0:T(8,128)(2,1)}, u32[]{:S(2)}) copy-start(bf16[1,64,2,64,256]{4,1,3,2,0:T(8,128)(2,1)} %get-tuple-element.23) | copy-start | bytes 12582916
  404.2 10.4 %copy-start.15 = (bf16[1,64,2,64,256]{4,1,3,2,0:T(8,128)(2,1)S(1)}, bf16[1,64,2,64,256]{4,1,3,2,0:T(8,128)(2,1)}, u32[]{:S(2)}) copy-start(bf16[1,64,2,64,256]{4,1,3,2,0:T(8,128)(2,1)} %get-tuple-element.20) | copy-start | bytes 12582916
  404.2 10.4 %copy-start.16 = (bf16[1,64,2,64,256]{4,1,3,2,0:T(8,128)(2,1)S(1)}, bf16[1,64,2,64,256]{4,1,3,2,0:T(8,128)(2,1)}, u32[]{:S(2)}) copy-start(bf16[1,64,2,64,256]{4,1,3,2,0:T(8,128)(2,1)} %get-tuple-element.21) | copy-start | bytes 12582916
  435.9 10.5 %copy-start.11 = (bf16[1,64,2,64,256]{4,1,3,2,0:T(8,128)(2,1)S(1)}, bf16[1,64,2,64,256]{4,1,3,2,0:T(8,128)(2,1)}, u32[]{:S(2)}) copy-start(bf16[1,64,2,64,256]{4,1,3,2,0:T(8,128)(2,1)} %get-tuple-element.16) | copy-start | bytes 12582916
  436.0 10.4 %copy-start.12 = (bf16[1,64,2,64,256]{4,1,3,2,0:T(8,128)(2,1)S(1)}, bf16[1,64,2,64,256]{4,1,3,2,0:T(8,128)(2,1)}, u32[]{:S(2)}) copy-start(bf16[1,64,2,64,256]{4,1,3,2,0:T(8,128)(2,1)} %get-tuple-element.17) | copy-start | bytes 12582916
  436.0 10.4 %copy-start.23 = (bf16[1,64,2,64,256]{4,1,3,2,0:T(8,128)(2,1)S(1)}, bf16[1,64,2,64,256]{4,1,3,2,0:T(8,128)(2,1)}, u32[]{:S(2)}) copy-start(bf16[1,64,2,64,256]{4,1,3,2,0:T(8,128)(2,1)} %get-tuple-element.31) | copy-start | bytes 12582916
  451.8 9.4 %copy-start.5 = (bf16[1,64,2,64,256]{4,1,3,2,0:T(8,128)(2,1)S(1)}, bf16[1,64,2,64,256]{4,1,3,2,0:T(8,128)(2,1)}, u32[]{:S(2)}) copy-start(bf16[1,64,2,64,256]{4,1,3,2,0:T(8,128)(2,1)} %get-tuple-element.41) | copy-start | bytes 12582916
  451.8 9.4 %copy-start.8 = (bf16[1,64,2,64,256]{4,1,3,2,0:T(8,128)(2,1)S(1)}, bf16[1,64,2,64,256]{4,1,3,2,0:T(8,128)(2,1)}, u32[]{:S(2)}) copy-start(bf16[1,64,2,64,256]{4,1,3,2,0:T(8,128)(2,1)} %get-tuple-element.14) | copy-start | bytes 12582916
  466.6 9.4 %copy-start.6 = (bf16[1,64,2,64,256]{4,1,3,2,0:T(8,128)(2,1)S(1)}, bf16[1,64,2,64,256]{4,1,3,2,0:T(8,128)(2,1)}, u32[]{:S(2)}) copy-start(bf16[1,64,2,64,256]{4,1,3,2,0:T(8,128)(2,1)} %get-tuple-element.13) | copy-start | bytes 12582916
  490.1 93.3 %copy-start.1 = (bf16[27,64]{1,0:T(8,128)(2,1)S(1)}, bf16[27,64]{1,0:T(8,128)(2,1)}, u32[]{:S(2)}) copy-start(bf16[27,64]{1,0:T(8,128)(2,1)} %param.13) | copy-start | bytes 10372
  (15 other events, 109.7 us)
Sparse Core Ops, SparseCore 0:
  11.5 10.3 reduce-scatter.3
  24.8 8.8 reduce-scatter.5
  111.9 5.4 reduce-scatter.7
  490.3 90.9 all-reduce.3
where the time goes:
time: 596 us; the launch traced here: 590 us
  matrix products  207 us (35%)
  local copies, waits for them, and re-layouts  121 us (20%)
  waiting for transfers between devices  93.5 us (16%)
  blocking collectives  60 us (10%)
  other arithmetic  56.7 us (10%)
  starting transfers between devices  36.9 us (6%)
  between operations  14.8 us (2%)
    dot_general x9, matrix products, shards(): jnp.einsum('izxy,dozxy->dio', act_in, stacked, preferred_element_type=jnp...  90.2 us
    another operation x4, local copies, waits for them, and re-layouts, shifted_windows(): return jnp.stack(windows, axis=0)  78.2 us
    psum x1, waiting for transfers between devices, shards(): lax.psum((grad_first, grad_second), ('wide', 'narrow'))  61.7 us
    psum x1, blocking collectives, shards(): lax.psum((grad_first, grad_second), ('wide', 'narrow'))  60 us
    dot_general x9, matrix products, shards(): jnp.einsum('dio,dozxy->izxy', w_first[plane_index::9], stacked, preferred...  53.7 us
    convert_element_type x1, other arithmetic, shards(): return (grad_in.astype(jnp.bfloat16), grad_first, grad_second)  25 us
    concatenate x6, other arithmetic, with_halo(): x = jnp.concatenate([before, x, after], axis=dim)  19.9 us
    unnamed x95, local copies, waits for them, and re-layouts  19.5 us
  transfers between devices with their start and end apart: 16, of which 10 were waited for; matrix products, arithmetic and copies ran while one was open for 12% of the time, Pallas kernels for 0%

commit v1 on v0

--- a/solution.py
+++ b/solution.py
@@ -149,7 +149,7 @@
             "dio,dozxy->izxy", w_first[plane_index::9], stacked, preferred_element_type=jnp.float32
         )
     grad_first = jnp.stack(first_parts, axis=1).reshape(27, channels, channels)
-    grad_first, grad_second = lax.psum((grad_first, grad_second), ("wide", "narrow"))
+    grad_first, grad_second = lax.psum(lax.psum((grad_first, grad_second), "narrow"), "wide")
     return (grad_in.astype(jnp.bfloat16), grad_first, grad_second)
 
 

time: 596 us -> 584 us (0.980)
  blocking collectives: 60 us -> 39.8 us
  matrix products: 207 us -> 216 us
    psum x1 -> x2, blocking collectives: 60 us -> 39.8 us  [the longest x1 36.5 us: shards(): lax.psum(lax.psum((grad_first, grad_second), 'narrow'), 'wide')]
    psum x1 -> x2, waiting for transfers between devices: 61.7 us -> 60.2 us  [the longest x1 51.2 us: shards(): lax.psum(lax.psum((grad_first, grad_second), 'narrow'), 'wide')]
  transfers between devices with their start and end apart: 16 -> 17, of which waited for: 10 -> 11; matrix products, arithmetic and copies ran while one was open for 12% -> 14% of each run, Pallas kernels for 0% -> 0%
where the time goes in v1:
time: 584 us; the launch traced here: 579 us
  matrix products  216 us (37%)
  local copies, waits for them, and re-layouts  122 us (21%)
  waiting for transfers between devices  92.1 us (16%)
  other arithmetic  56.7 us (10%)
  blocking collectives  39.8 us (7%)
  starting transfers between devices  36.8 us (6%)
  between operations  14.9 us (3%)
    dot_general x9, matrix products, shards(): jnp.einsum('izxy,dozxy->dio', act_in, stacked, preferred_element_type=jnp...  96.1 us
    another operation x4, local copies, waits for them, and re-layouts, shifted_windows(): return jnp.stack(windows, axis=0)  78.2 us
    dot_general x9, matrix products, shards(): jnp.einsum('dio,dozxy->izxy', w_first[plane_index::9], stacked, preferred...  56.7 us
    psum x1, waiting for transfers between devices, shards(): lax.psum(lax.psum((grad_first, grad_second), 'narrow'), 'wide')  51.2 us
    psum x1, blocking collectives, shards(): lax.psum(lax.psum((grad_first, grad_second), 'narrow'), 'wide')  36.5 us
    convert_element_type x1, other arithmetic, shards(): return (grad_in.astype(jnp.bfloat16), grad_first, grad_second)  25.1 us
    unnamed x95, local copies, waits for them, and re-layouts  20.2 us
    concatenate x6, other arithmetic, with_halo(): x = jnp.concatenate([before, x, after], axis=dim)  19.9 us
  transfers between devices with their start and end apart: 17, of which 11 were waited for; matrix products, arithmetic and copies ran while one was open for 14% of the time, Pallas kernels for 0%

profile of v1, /device:TPU:0, one launch (start us, length us, event | category | flops | bytes accessed | tf_op | source)
XLA Modules:
  0.0 578.8 jit_solution(2518009259612662557)
XLA Ops:
  15.5 6.4 %reduce-scatter.4.cloned.1.call-done = f32[2,64,256]{2,1,0:T(8,128)} async-done(((f32[2,64,512]{2,1,0:T(8,128)}), f32[2,64,256]{2,1,0:T(8,128)}) %reduce-scatter.4.cloned.1.call-update) | async-done | bytes 131088 | tf_op jit(solution)/shard_map/reduce_scatter | solution.py:64
  23.8 5.7 all-to-all-start
  64.7 5.3 fusion.45
  99.1 6.0 %all-to-all-done.3 = f32[8,1,4096]{2,1,0:T(1,128)S(1)} async-done(((f32[8,1,4096]{2,1,0:T(1,128)}), f32[8,1,4096]{2,1,0:T(1,128)S(1)}, u32[]{:S(2)}, u32[]{:S(2)}) %all-to-all-start.3) | async-done | bytes 131104 | tf_op jit(solution)/shard_map/all_to_all | solution.py:109
  112.0 5.5 reduce-scatter.8.cloned.1.call-done
  147.6 6.3 %fusion.100 = f32[27,64]{1,0:T(8,128)S(1)} fusion(bf16[64,2,64,256]{3,2,1,0:T(8,128)(2,1)S(1)} %copy-done.28, bf16[27,2,64,256]{3,2,1,0:T(8,128)(2,1)S(1)} %constant_dynamic-update-slice_fusion), kind=kOutput, calls=%fused_computation.124 | convolution fusion | flops 113246208 | bytes 5970688 | tf_op jit(solution)/shard_map/czxy,tzxy->tc/dot_general | solution.py:134
  157.3 36.5 %psum.31 = f32[27,64]{1,0:T(8,128)} all-reduce(f32[27,64]{1,0:T(8,128)S(1)} %psum.30), channel_id=1, replica_groups=mesh['grp'=2,'wide'=8,'narrow'=2] {'wide'}, use_global_device_ids=true, to_apply=%region_6.7 | all-reduce | flops 1728 | bytes 13824 | tf_op jit(solution)/shard_map/psum | solution.py:152
  207.9 5.8 %fusion.27 = (bf16[1,64,2,64,256]{4,1,3,2,0:T(8,128)(2,1)}, bf16[1,64,2,64,256]{4,1,3,2,0:T(8,128)(2,1)}) fusion(bf16[64,2,1,256]{3,0,2,1:T(8,128)(2,1)S(1)} %collective-permute-done.5, bf16[64,2,64,256]{3,0,2,1:T(8,128)(2,1)} %copy-done.2, bf16[64,2,1,256]{3,0,2,1:T(8,128)(2,1)S(1)} %collective-permute-done.4), kind=kLoop, calls=%fused_computation.74 | loop fusion | flops 4194304 | bytes 12713984 | tf_op jit(solution)/shard_map/stack | solution.py:43
  222.7 8.2 %pad_maximum_fusion.9 = (bf16[64,2,66,257]{3,0,2,1:T(8,128)(2,1)S(1)}, bf16[64,2,66,257]{3,0,2,1:T(8,128)(2,1)S(1)}) fusion(bf16[64,2,66,1]{3,0,2,1:T(8,128)(2,1)} %copy.104, bf16[64,2,1,256]{3,0,2,1:T(8,128)(2,1)S(1)} %collective-permute-done.5, bf16[64,2,64,256]{3,0,2,1:T(8,128)(2,1)} %copy-done.2, bf16[64,2,1,256]{3,0,2,1:T(8,128)(2,1)S(1)} %collective-permute-done.4, ...), kind=kLoop, calls=%fused_computation.30 | loop fusion | flops 34738176 | bytes 13043712 | tf_op jit(solution)/shard_map/concatenate | solution.py:19
  230.9 9.2 %slice_bitcast_fusion.22 = (bf16[1,64,2,64,256]{4,1,3,2,0:T(8,128)(2,1)}, bf16[1,64,2,64,256]{4,1,3,2,0:T(8,128)(2,1)}, bf16[1,64,2,64,256]{4,1,3,2,0:T(8,128)(2,1)}) fusion(bf16[64,2,66,257]{3,0,2,1:T(8,128)(2,1)S(1)} %get-tuple-element.36), kind=kLoop, calls=%fused_computation.77 | loop fusion | bytes 25165824 | tf_op jit(solution)/shard_map/stack | solution.py:43
  240.1 9.0 %select_maximum_fusion = bf16[64,4,66,258]{3,0,2,1:T(8,128)(2,1)} fusion(bf16[64,2,66,1]{3,0,2,1:T(8,128)(2,1)} %copy.104, bf16[64,2,66,1]{3,0,2,1:T(8,128)(2,1)S(1)} %copy-done.4, bf16[64,2,1,256]{3,0,2,1:T(8,128)(2,1)S(1)} %collective-permute-done.5, bf16[64,2,64,256]{3,0,2,1:T(8,128)(2,1)S(1)} %copy-done.3, ...), kind=kLoop, calls=%fused_computation.3 | loop fusion | flops 78465024 | bytes 13077504 | tf_op jit(solution)/shard_map/concatenate | solution.py:19
  249.0 64.1 %slice_bitcast_fusion.23 = (bf16[1,64,2,64,256]{4,1,3,2,0:T(8,128)(2,1)}, bf16[1,64,2,64,256]{4,1,3,2,0:T(8,128)(2,1)}, bf16[1,64,2,64,256]{4,1,3,2,0:T(8,128)(2...) fusion(bf16[64,4,66,258]{3,0,2,1:T(8,128)(2,1)} %select_maximum, ...), kind=kLoop, calls=%fused_computation.78 | loop fusion | bytes 150994944 | tf_op jit(solution)/shard_map/stack | solution.py:43
  313.1 14.6 %fusion.49 = f32[3,9,64,64]{2,3,0,1:T(8,128)S(1)} fusion(bf16[1,64,2,64,256]{4,1,3,2,0:T(8,128)(2,1)} %get-tuple-element.28, bf16[1,64,2,64,256]{4,1,3,2,0:T(8,128)(2,1)} %get-tuple-element.30, bf16[1,64,2,64,256]{4,1,3,2,0:T(8,128)(2,1)} %get-tuple-element.12, bf16[64,2,64,256,1]{3,2,1,0,4:T(8,128)(2,1)} %bitcast.559), kind=kOutput, calls=%fused_computation.107 | convolution fusion | flops 817889280 | bytes 16875520 | tf_op jit(solution)/shard_map/izxy,dozxy->dio/dot_general | solution.py:146
  327.8 8.5 %fusion.25 = f32[2,64,256,64,1]{2,3,1,0,4:T(8,128)} fusion(bf16[1,64,2,64,256]{4,1,3,2,0:T(8,128)(2,1)} %get-tuple-element.28, bf16[1,64,2,64,256]{4,1,3,2,0:T(8,128)(2,1)} %get-tuple-element.30, bf16[1,64,2,64,256]{4,1,3,2,0:T(8,128)(2,1)} %get-tuple-element.12, bf16[27,64,64]{2,1,0:T(8,128)(2,1)S(1)} %copy-done.29), kind=kOutput, calls=%fused_computation.49 | convolution fusion | flops 843055104 | bytes 21020672 | tf_op jit(solution)/shard_map/dio,dozxy->izxy/dot_general | solution.py:148
  344.1 10.0 %fusion.55 = f32[3,9,64,64]{2,3,0,1:T(8,128)S(1)} fusion(f32[3,9,64,64]{2,3,0,1:T(8,128)S(1)} %fusion.49, bf16[1,64,2,64,256]{4,1,3,2,0:T(8,128)(2,1)S(1)} %copy-done.21, bf16[1,64,2,64,256]{4,1,3,2,0:T(8,128)(2,1)S(1)} %copy-done.10, bf16[1,64,2,64,256]{4,1,3,2,0:T(8,128)(2,1)S(1)} %copy-done.22, bf16[64,2,64,256,1]{3,2,1,0,4:T(8,128)(2,1)} %bitcast.560), kind=kOutput, calls=%fused_computation.109 | convolution fusion | flops 817889280 | bytes 16875520 | tf_op jit(solution)/shard_map/izxy,dozxy->dio/dot_general | solution.py:146
  361.6 5.3 fusion.21
  366.9 11.4 %fusion.61 = f32[3,9,64,64]{2,3,0,1:T(8,128)S(1)} fusion(f32[3,9,64,64]{2,3,0,1:T(8,128)S(1)} %fusion.55, bf16[1,64,2,64,256]{4,1,3,2,0:T(8,128)(2,1)S(1)} %copy-done.19, bf16[1,64,2,64,256]{4,1,3,2,0:T(8,128)(2,1)} %copy-done.26, bf16[1,64,2,64,256]{4,1,3,2,0:T(8,128)(2,1)S(1)} %copy-done.20, bf16[64,2,64,256,1]{3,2,1,0,4:T(8,128)(2,1)} %bitcast.561), kind=kOutput, calls=%fused_computation.111 | convolution fusion | flops 817889280 | bytes 16875520 | tf_op jit(solution)/shard_map/izxy,dozxy->dio/dot_general | solution.py:146
  378.3 6.8 %fusion.19 = f32[2,64,256,64,1]{2,3,1,0,4:T(8,128)} fusion(bf16[1,64,2,64,256]{4,1,3,2,0:T(8,128)(2,1)S(1)} %copy-done.17, bf16[1,64,2,64,256]{4,1,3,2,0:T(8,128)(2,1)} %get-tuple-element.32, bf16[1,64,2,64,256]{4,1,3,2,0:T(8,128)(2,1)S(1)} %copy-done.18, bf16[27,64,64]{2,1,0:T(8,128)(2,1)S(1)} %copy-done.29), kind=kOutput, calls=%fused_computation.43 | convolution fusion | flops 843055104 | bytes 21020672 | tf_op jit(solution)/shard_map/dio,dozxy->izxy/dot_general | solution.py:148
  385.2 11.5 %fusion.67 = f32[3,9,64,64]{2,3,0,1:T(8,128)S(1)} fusion(f32[3,9,64,64]{2,3,0,1:T(8,128)S(1)} %fusion.61, bf16[1,64,2,64,256]{4,1,3,2,0:T(8,128)(2,1)S(1)} %copy-done.17, bf16[1,64,2,64,256]{4,1,3,2,0:T(8,128)(2,1)} %get-tuple-element.32, bf16[1,64,2,64,256]{4,1,3,2,0:T(8,128)(2,1)S(1)} %copy-done.18, bf16[64,2,64,256,1]{3,2,1,0,4:T(8,128)(2,1)} %bitcast.562), kind=kOutput, calls=%fused_computation.113 | convolution fusion | flops 817889280 | bytes 16875520 | tf_op jit(solution)/shard_map/izxy,dozxy->dio/dot_general | solution.py:146
  396.7 5.3 fusion.17
  402.0 10.3 %fusion.73 = f32[3,9,64,64]{2,3,0,1:T(8,128)S(1)} fusion(f32[3,9,64,64]{2,3,0,1:T(8,128)S(1)} %fusion.67, bf16[1,64,2,64,256]{4,1,3,2,0:T(8,128)(2,1)S(1)} %copy-done.15, bf16[1,64,2,64,256]{4,1,3,2,0:T(8,128)(2,1)S(1)} %bitcast.549, bf16[1,64,2,64,256]{4,1,3,2,0:T(8,128)(2,1)S(1)} %copy-done.16, bf16[64,2,64,256,1]{3,2,1,0,4:T(8,128)(2,1)} %bitcast.563), kind=kOutput, calls=%fused_computation.115 | convolution fusion | flops 817889280 | bytes 16875520 | tf_op jit(solution)/shard_map/izxy,dozxy->dio/dot_general | solution.py:146
  413.3 6.6 %fusion.15 = f32[2,64,256,64,1]{2,3,1,0,4:T(8,128)} fusion(bf16[1,64,2,64,256]{4,1,3,2,0:T(8,128)(2,1)S(1)} %copy-done.13, bf16[1,64,2,64,256]{4,1,3,2,0:T(8,128)(2,1)} %get-tuple-element.35, bf16[1,64,2,64,256]{4,1,3,2,0:T(8,128)(2,1)S(1)} %copy-done.14, bf16[27,64,64]{2,1,0:T(8,128)(2,1)S(1)} %copy-done.29), kind=kOutput, calls=%fused_computation.39 | convolution fusion | flops 843055104 | bytes 21020672 | tf_op jit(solution)/shard_map/dio,dozxy->izxy/dot_general | solution.py:148
  419.9 10.4 %fusion.79 = f32[3,9,64,64]{2,3,0,1:T(8,128)} fusion(f32[3,9,64,64]{2,3,0,1:T(8,128)} %copy-done.27, bf16[1,64,2,64,256]{4,1,3,2,0:T(8,128)(2,1)S(1)} %copy-done.13, bf16[1,64,2,64,256]{4,1,3,2,0:T(8,128)(2,1)} %get-tuple-element.35, bf16[1,64,2,64,256]{4,1,3,2,0:T(8,128)(2,1)S(1)} %copy-done.14, bf16[64,2,64,256,1]{3,2,1,0,4:T(8,128)(2,1)} %bitcast.564), kind=kOutput, calls=%fused_computation.117 | convolution fusion | flops 817889280 | bytes 16875520 | tf_op jit(solution)/shard_map/izxy,dozxy->dio/dot_general | solution.py:146
  430.3 5.3 fusion.13
  435.7 9.3 %fusion.85 = f32[3,9,64,64]{2,3,0,1:T(8,128)} fusion(f32[3,9,64,64]{2,3,0,1:T(8,128)} %fusion.79, bf16[1,64,2,64,256]{4,1,3,2,0:T(8,128)(2,1)S(1)} %copy-done.11, bf16[1,64,2,64,256]{4,1,3,2,0:T(8,128)(2,1)S(1)} %copy-done.24, bf16[1,64,2,64,256]{4,1,3,2,0:T(8,128)(2,1)S(1)} %copy-done.12, bf16[64,2,64,256,1]{3,2,1,0,4:T(8,128)(2,1)} %bitcast.565), kind=kOutput, calls=%fused_computation.119 | convolution fusion | flops 817889280 | bytes 16875520 | tf_op jit(solution)/shard_map/izxy,dozxy->dio/dot_general | solution.py:146
  445.0 5.4 fusion.11
  450.5 9.3 %fusion.91 = f32[3,9,64,64]{2,3,0,1:T(8,128)} fusion(f32[3,9,64,64]{2,3,0,1:T(8,128)} %fusion.85, bf16[1,64,2,64,256]{4,1,3,2,0:T(8,128)(2,1)S(1)} %copy-done.8, bf16[1,64,2,64,256]{4,1,3,2,0:T(8,128)(2,1)S(1)} %copy-done.5, bf16[1,64,2,64,256]{4,1,3,2,0:T(8,128)(2,1)S(1)} %copy-done.9, bf16[64,2,64,256,1]{3,2,1,0,4:T(8,128)(2,1)} %bitcast.566), kind=kOutput, calls=%fused_computation.121 | convolution fusion | flops 817889280 | bytes 16875520 | tf_op jit(solution)/shard_map/izxy,dozxy->dio/dot_general | solution.py:146
  459.9 9.2 %fusion.97 = f32[3,9,64,64]{2,3,0,1:T(8,128)} fusion(f32[3,9,64,64]{2,3,0,1:T(8,128)} %fusion.91, bf16[1,64,2,64,256]{4,1,3,2,0:T(8,128)(2,1)S(1)} %copy-done.7, bf16[1,64,2,64,256]{4,1,3,2,0:T(8,128)(2,1)S(1)} %copy-done.25, bf16[1,64,2,64,256]{4,1,3,2,0:T(8,128)(2,1)S(1)} %copy-done.6, bf16[64,2,64,256,1]{3,2,1,0,4:T(8,128)(2,1)} %bitcast.567), kind=kOutput, calls=%fused_computation.123 | convolution fusion | flops 817889280 | bytes 16875520 | tf_op jit(solution)/shard_map/izxy,dozxy->dio/dot_general | solution.py:146
  471.7 8.4 %fusion.9 = f32[2,64,256,64,1]{2,3,1,0,4:T(8,128)} fusion(bf16[1,64,2,64,256]{4,1,3,2,0:T(8,128)(2,1)} %get-tuple-element.29, bf16[1,64,2,64,256]{4,1,3,2,0:T(8,128)(2,1)} %get-tuple-element.34, bf16[1,64,2,64,256]{4,1,3,2,0:T(8,128)(2,1)} %get-tuple-element.13, bf16[27,64,64]{2,1,0:T(8,128)(2,1)S(1)} %copy-done.29), kind=kOutput, calls=%fused_computation.33 | convolution fusion | flops 843055104 | bytes 21020672 | tf_op jit(solution)/shard_map/dio,dozxy->izxy/dot_general | solution.py:148
  480.1 9.1 %all-reduce.5.cloned.1.call-done = f32[27,64,64]{2,1,0:T(8,128)} async-done(((f32[27,64,64]{2,1,0:T(8,128)}), f32[27,64,64]{2,1,0:T(8,128)}) %all-reduce.5.cloned.1.call-update) | async-done | bytes 442384 | tf_op jit(solution)/shard_map/psum | solution.py:152
  489.2 25.1 %fusion.39 = bf16[64,2,64,256]{3,0,1,2:T(8,128)(2,1)S(1)} fusion(f32[2,64,256,64,1]{2,3,1,0,4:T(8,128)} %fusion.9, f32[2,64,256,64,1]{2,3,1,0,4:T(8,128)} %fusion.11, f32[2,64,256,64,1]{2,3,1,0,4:T(8,128)} %fusion.13, f32[2,64,256,64,1]{2,3,1,0,4:T(8,128)} %fusion.15, f32[2,64,256,64,1]{2,3,1,0,4:T(8,128)} %fusion.17, f32[2,64,256,64,1]{2,3,1,0,4:T(8,128)} %fusion.19, ...), kind=kLoop, calls=%fused_computation.90 | loop fusion | flops 18874368 | bytes 79691776 | tf_op jit(solution)/shard_map/convert_element_type | solution.py:153
  518.7 51.2 %all-reduce.7.cloned.1.call-done = f32[27,64,64]{2,1,0:T(8,128)} async-done(((f32[27,64,64]{2,1,0:T(8,128)}), f32[27,64,64]{2,1,0:T(8,128)}) %all-reduce.7.cloned.1.call-update) | async-done | bytes 442384 | tf_op jit(solution)/shard_map/psum | solution.py:152
  (187 shorter events, 163.0 us)
Async XLA Ops:
  7.2 128.1 %copy-start = (bf16[27,64]{1,0:T(8,128)(2,1)S(1)}, bf16[27,64]{1,0:T(8,128)(2,1)}, u32[]{:S(2)}) copy-start(bf16[27,64]{1,0:T(8,128)(2,1)} %param.13) | copy-start | bytes 10372
  7.2 14.7 %reduce-scatter.4.cloned.1.call-start = ((), (), s32[]{:S(2)}) async-start(), calls=%async_computation.7 | async-start | bytes 393216 | tf_op jit(solution)/shard_map/reduce_scatter | solution.py:64
  11.4 22.3 %reduce-scatter.6.cloned.1.call-start = ((), (), s32[]{:S(2)}) async-start(), calls=%async_computation.8 | async-start | bytes 393216 | tf_op jit(solution)/shard_map/reduce_scatter | solution.py:65
  23.8 13.2 %all-to-all-start = ((f32[8,1,4096]{2,1,0:T(1,128)}), f32[8,1,4096]{2,1,0:T(1,128)S(1)}, u32[]{:S(2)}, u32[]{:S(2)}) async-start(f32[8,1,4096]{2,1,0:T(1,128)} %reshape.165), calls=%async_computation.1 | async-start | bytes 262144 | tf_op jit(solution)/shard_map/all_to_all | solution.py:70
  37.0 12.0 %all-to-all-start.1 = ((f32[8,1,4096]{2,1,0:T(1,128)}), f32[8,1,4096]{2,1,0:T(1,128)S(1)}, u32[]{:S(2)}, u32[]{:S(2)}) async-start(f32[8,1,4096]{2,1,0:T(1,128)} %reshape.167), calls=%async_computation.3 | async-start | bytes 262144 | tf_op jit(solution)/shard_map/all_to_all | solution.py:77
  80.7 12.6 %all-to-all-start.2 = ((f32[8,1,4096]{2,1,0:T(1,128)}), f32[8,1,4096]{2,1,0:T(1,128)S(1)}, u32[]{:S(2)}, u32[]{:S(2)}) async-start(f32[8,1,4096]{2,1,0:T(1,128)} %reshape.169), calls=%async_computation.4 | async-start | bytes 262144 | tf_op jit(solution)/shard_map/all_to_all | solution.py:102
  93.2 11.8 %all-to-all-start.3 = ((f32[8,1,4096]{2,1,0:T(1,128)}), f32[8,1,4096]{2,1,0:T(1,128)S(1)}, u32[]{:S(2)}, u32[]{:S(2)}) async-start(f32[8,1,4096]{2,1,0:T(1,128)} %reshape.171), calls=%async_computation.5 | async-start | bytes 262144 | tf_op jit(solution)/shard_map/all_to_all | solution.py:109
  97.7 19.8 %reduce-scatter.8.cloned.1.call-start = ((), (), s32[]{:S(2)}) async-start(), calls=%async_computation.9 | async-start | bytes 393216 | tf_op jit(solution)/shard_map/reduce_scatter | solution.py:124
  111.9 377.2 %all-reduce.5.cloned.1.call-start = ((), (), s32[]{:S(2)}) async-start(), calls=%async_computation.10 | async-start | bytes 1769472 | tf_op jit(solution)/shard_map/psum | solution.py:152
  117.5 17.8 %copy-start.28 = (bf16[64,2,64,256]{3,2,1,0:T(8,128)(2,1)S(1)}, bf16[64,2,64,256]{3,2,1,0:T(8,128)(2,1)}, u32[]{:S(2)}) copy-start(bf16[64,2,64,256]{3,2,1,0:T(8,128)(2,1)} %param.11) | copy-start | bytes 12582916
  118.6 5.0 collective-permute-start
  122.4 5.5 collective-permute-start.1
  127.9 2.6 collective-permute-start.2
  129.2 3.1 collective-permute-start.3
  141.8 52.0 %collective-permute-start.4 = (bf16[64,2,1,256]{3,0,2,1:T(8,128)(2,1)S(1)}, bf16[64,2,1,256]{3,0,2,1:T(8,128)(2,1)S(1)}, u32[]{:S(2)}, u32[]{:S(2)}) collective-permute-start(bf16[64,2,1,256]{3,0,2,1:T(8,128)(2,1)S(1)} %get-tuple-element.42), channel_id=1, source_target_pairs={{0,2},{2,4},{4,6},{6,8},{8,10},{10,12},{12,14},{1,3},{3,5},{5,7},{... | collective-permute-start | bytes 196616 | tf_op jit(solution)/shard_map/ppermute | solution.py:17
  146.1 47.7 %collective-permute-start.5 = (bf16[64,2,1,256]{3,0,2,1:T(8,128)(2,1)S(1)}, bf16[64,2,1,256]{3,0,2,1:T(8,128)(2,1)S(1)}, u32[]{:S(2)}, u32[]{:S(2)}) collective-permute-start(bf16[64,2,1,256]{3,0,2,1:T(8,128)(2,1)S(1)} %get-tuple-element.43), channel_id=1, source_target_pairs={{2,0},{4,2},{6,4},{8,6},{10,8},{12,10},{14,12},{3,1},{5,3},{7,5},{... | collective-permute-start | bytes 196616 | tf_op jit(solution)/shard_map/ppermute | solution.py:18
  202.4 11.3 %collective-permute-start.6 = (bf16[64,2,66,1]{2,0,3,1:T(8,128)(2,1)S(1)}, bf16[64,2,66,1]{2,0,3,1:T(8,128)(2,1)S(1)}, u32[]{:S(2)}, u32[]{:S(2)}) collective-permute-start(bf16[64,2,66,1]{2,0,3,1:T(8,128)(2,1)S(1)} %copy.101), channel_id=1, source_target_pairs={{0,1},{2,3},{4,5},{6,7},{8,9},{10,11},{12,13},{14,15},{16,17},{18,... | collective-permute-start | bytes 50696 | tf_op jit(solution)/shard_map/ppermute | solution.py:17
  206.2 12.0 %collective-permute-start.7 = (bf16[64,2,66,1]{2,0,3,1:T(8,128)(2,1)S(1)}, bf16[64,2,66,1]{2,0,3,1:T(8,128)(2,1)S(1)}, u32[]{:S(2)}, u32[]{:S(2)}) collective-permute-start(bf16[64,2,66,1]{2,0,3,1:T(8,128)(2,1)S(1)} %copy.102), channel_id=1, source_target_pairs={{1,0},{3,2},{5,4},{7,6},{9,8},{11,10},{13,12},{15,14},{17,16},{19,... | collective-permute-start | bytes 50696 | tf_op jit(solution)/shard_map/ppermute | solution.py:18
  313.1 14.6 %copy-start.29 = (bf16[27,64,64]{2,1,0:T(8,128)(2,1)S(1)}, bf16[27,64,64]{2,1,0:T(8,128)(2,1)}, u32[]{:S(2)}) copy-start(bf16[27,64,64]{2,1,0:T(8,128)(2,1)} %param.12) | copy-start | bytes 663556
  327.7 10.0 %copy-start.21 = (bf16[1,64,2,64,256]{4,1,3,2,0:T(8,128)(2,1)S(1)}, bf16[1,64,2,64,256]{4,1,3,2,0:T(8,128)(2,1)}, u32[]{:S(2)}) copy-start(bf16[1,64,2,64,256]{4,1,3,2,0:T(8,128)(2,1)} %get-tuple-element.26) | copy-start | bytes 12582916
  327.7 11.2 %copy-start.22 = (bf16[1,64,2,64,256]{4,1,3,2,0:T(8,128)(2,1)S(1)}, bf16[1,64,2,64,256]{4,1,3,2,0:T(8,128)(2,1)}, u32[]{:S(2)}) copy-start(bf16[1,64,2,64,256]{4,1,3,2,0:T(8,128)(2,1)} %get-tuple-element.27) | copy-start | bytes 12582916
  366.9 11.4 %copy-start.17 = (bf16[1,64,2,64,256]{4,1,3,2,0:T(8,128)(2,1)S(1)}, bf16[1,64,2,64,256]{4,1,3,2,0:T(8,128)(2,1)}, u32[]{:S(2)}) copy-start(bf16[1,64,2,64,256]{4,1,3,2,0:T(8,128)(2,1)} %get-tuple-element.22) | copy-start | bytes 12582916
  366.9 11.4 %copy-start.18 = (bf16[1,64,2,64,256]{4,1,3,2,0:T(8,128)(2,1)S(1)}, bf16[1,64,2,64,256]{4,1,3,2,0:T(8,128)(2,1)}, u32[]{:S(2)}) copy-start(bf16[1,64,2,64,256]{4,1,3,2,0:T(8,128)(2,1)} %get-tuple-element.23) | copy-start | bytes 12582916
  385.2 11.5 %copy-start.15 = (bf16[1,64,2,64,256]{4,1,3,2,0:T(8,128)(2,1)S(1)}, bf16[1,64,2,64,256]{4,1,3,2,0:T(8,128)(2,1)}, u32[]{:S(2)}) copy-start(bf16[1,64,2,64,256]{4,1,3,2,0:T(8,128)(2,1)} %get-tuple-element.20) | copy-start | bytes 12582916
  385.2 11.5 %copy-start.16 = (bf16[1,64,2,64,256]{4,1,3,2,0:T(8,128)(2,1)S(1)}, bf16[1,64,2,64,256]{4,1,3,2,0:T(8,128)(2,1)}, u32[]{:S(2)}) copy-start(bf16[1,64,2,64,256]{4,1,3,2,0:T(8,128)(2,1)} %get-tuple-element.21) | copy-start | bytes 12582916
  402.0 11.3 %copy-start.13 = (bf16[1,64,2,64,256]{4,1,3,2,0:T(8,128)(2,1)S(1)}, bf16[1,64,2,64,256]{4,1,3,2,0:T(8,128)(2,1)}, u32[]{:S(2)}) copy-start(bf16[1,64,2,64,256]{4,1,3,2,0:T(8,128)(2,1)} %get-tuple-element.18) | copy-start | bytes 12582916
  402.0 11.3 %copy-start.14 = (bf16[1,64,2,64,256]{4,1,3,2,0:T(8,128)(2,1)S(1)}, bf16[1,64,2,64,256]{4,1,3,2,0:T(8,128)(2,1)}, u32[]{:S(2)}) copy-start(bf16[1,64,2,64,256]{4,1,3,2,0:T(8,128)(2,1)} %get-tuple-element.19) | copy-start | bytes 12582916
  419.9 10.5 %copy-start.11 = (bf16[1,64,2,64,256]{4,1,3,2,0:T(8,128)(2,1)S(1)}, bf16[1,64,2,64,256]{4,1,3,2,0:T(8,128)(2,1)}, u32[]{:S(2)}) copy-start(bf16[1,64,2,64,256]{4,1,3,2,0:T(8,128)(2,1)} %get-tuple-element.16) | copy-start | bytes 12582916
  419.9 10.4 %copy-start.12 = (bf16[1,64,2,64,256]{4,1,3,2,0:T(8,128)(2,1)S(1)}, bf16[1,64,2,64,256]{4,1,3,2,0:T(8,128)(2,1)}, u32[]{:S(2)}) copy-start(bf16[1,64,2,64,256]{4,1,3,2,0:T(8,128)(2,1)} %get-tuple-element.17) | copy-start | bytes 12582916
  419.9 10.4 %copy-start.23 = (bf16[1,64,2,64,256]{4,1,3,2,0:T(8,128)(2,1)S(1)}, bf16[1,64,2,64,256]{4,1,3,2,0:T(8,128)(2,1)}, u32[]{:S(2)}) copy-start(bf16[1,64,2,64,256]{4,1,3,2,0:T(8,128)(2,1)} %get-tuple-element.31) | copy-start | bytes 12582916
  471.6 98.2 %all-reduce.7.cloned.1.call-start = ((), (), s32[]{:S(2)}) async-start(), calls=%async_computation.11 | async-start | bytes 1769472 | tf_op jit(solution)/shard_map/psum | solution.py:152
  489.2 82.9 %copy-start.1 = (bf16[27,64]{1,0:T(8,128)(2,1)S(1)}, bf16[27,64]{1,0:T(8,128)(2,1)}, u32[]{:S(2)}) copy-start(bf16[27,64]{1,0:T(8,128)(2,1)} %param.13) | copy-start | bytes 10372
  (16 other events, 114.7 us)
Sparse Core Ops, SparseCore 0:
  11.5 10.3 reduce-scatter.3
  24.8 8.8 reduce-scatter.5
  112.0 5.4 reduce-scatter.7
  471.8 17.3 all-reduce.4
  492.8 76.9 all-reduce.6
